TPU v7x, 32 devices: a whole 2x2x4 slice. The times are simulated.
32 devices in a mesh: groups: 2 (over x), long: 16 (over z, y, core).
Axes of the slice: x: 2, y: 2, z: 4, core: 2. Of those that a mesh axis runs over, the one named last changes fastest.
Arguments:
- displacement: float32 [4, 2, 128, 16, 256], P('groups', None, 'long'), parts along dimension 0, may hold values from -6 to 6
- velocity: float32 [4, 2, 128, 16, 256], P('groups', None, 'long'), parts along dimension 0, may hold values from -4 to 4
- damage: float32 [4, 128, 16, 256], P('groups', 'long'), parts along dimension 0, may hold values from 0 to 0.6
- material: int32 [4, 128, 16, 256], P('groups', 'long'), parts along dimension 0, may hold values from 0 to 3
- damage_table: float32 [2, 4], replicated, may hold values from 0.1 to 2
- fault_rows: int32 [4, 128, 16], P('groups', 'long'), parts along dimension 0, may hold values from 0 to 3
- kernel: float32 [16, 64, 2, 2], P(None, 'long'), may hold values from -1.5 to 1.5
- history: float32 [30, 64, 2, 2, 16], P('groups', 'long'), parts along dimension 0, may hold values from -6 to 6
Outputs:
- displacement_out: float32 [4, 2, 128, 16, 256], P('groups', None, 'long'), parts along dimension 0
- velocity_out: float32 [4, 2, 128, 16, 256], P('groups', None, 'long'), parts along dimension 0
- damage_out: float32 [4, 128, 16, 256], P('groups', 'long'), parts along dimension 0
- history_out: float32 [30, 64, 2, 2, 16], P('groups', 'long'), parts along dimension 0
There are 2 independent parts, one for each index of `groups`. A program takes and returns all parts, laid end to end along the dimension named above; an argument that names none is the same for every part. Nothing has to cross between parts.
Inputs may be any that keep to these rules, and one draw needn't show every extreme that they name: `fault_rows`: row of the fault face, counted from the fault.
All inputs are finite; a program needn't handle non-finite values.
Results may differ from a plain program's by a relative error of at most 0.00011.
Values sent between devices are 32-bit elements; how exact they have to be, the bound alone decides.
A program may use at most 64 MiB of HBM per device.

v0:
```python
import math
import jax
import jax.numpy as jnp
from jax import lax
from jax.sharding import PartitionSpec as P

STEPS = 2
time_step = 0.5


def padded_2(block, sides, width):
    for axis, dim in sides:
        count = lax.axis_size(axis)
        forward = [(i, i + 1) for i in range(count - 1)]
        forward.append((count - 1, 0))
        backward = [(target, source) for source, target in forward]
        low = lax.ppermute(
            lax.slice_in_dim(block, block.shape[dim] - width, None, axis=dim), axis, forward
        )
        high = lax.ppermute(lax.slice_in_dim(block, 0, width, axis=dim), axis, backward)
        block = jnp.concatenate([low, block, high], axis=dim)
    return block


def class_lookup(material, table_row):
    result = jnp.zeros(material.shape, table_row.dtype)
    for level in range(table_row.shape[0]):
        result = result + jnp.where(
            material == level, table_row[level], jnp.zeros((), table_row.dtype)
        )
    return result


def neighbour(values_in, axis, higher):
    selector = [slice(None)] * values_in.ndim
    for dimension in range(values_in.ndim - 3, values_in.ndim):
        selector[dimension] = slice(1, -1)
    selector[axis] = slice(2, None) if higher else slice(0, -2)
    return values_in[tuple(selector)]


def local_terms(padded_u, padded_c):
    outer_u = jnp.pad(padded_u, ((0, 0), (0, 0), (0, 0), (1, 1), (1, 1)))
    outer_c = jnp.pad(padded_c, ((0, 0), (0, 0), (1, 1), (1, 1)), mode="edge")
    centre_u = outer_u[:, :, 1:-1, 1:-1, 1:-1]
    centre_c = outer_c[:, 1:-1, 1:-1, 1:-1]
    forces = jnp.zeros_like(centre_u)
    energy = jnp.zeros_like(centre_c)
    for offset in range(3):
        above_u = neighbour(outer_u, 2 + offset, True)
        below_u = neighbour(outer_u, 2 + offset, False)
        above_c = neighbour(outer_c, 1 + offset, True)
        below_c = neighbour(outer_c, 1 + offset, False)
        forces = forces + (0.5 * (centre_c + above_c))[None] * (above_u - centre_u)
        forces = forces + (0.5 * (centre_c + below_c))[None] * (below_u - centre_u)
        gradient = 0.5 * (above_u - below_u)
        energy = energy + jnp.sum(gradient * gradient, axis=0)
    return (forces, energy)


def convolve(kernel, stacked):
    kernel_real = kernel[:, :, 0, :, None]
    kernel_imag = kernel[:, :, 1, :, None]
    spec_real = stacked[:, :, 0]
    spec_imag = stacked[:, :, 1]
    out_real = jnp.sum(kernel_real * spec_real - kernel_imag * spec_imag, axis=0)
    out_imag = jnp.sum(kernel_real * spec_imag + kernel_imag * spec_real, axis=0)
    return (out_real, out_imag)


def basis(waves, places, length):
    phase = (waves[:, None] * places[None, :] % length).astype(jnp.float32) * (
        2.0 * math.pi / length
    )
    return (jnp.cos(phase), jnp.sin(phase))


def spectral_terms(cosine, sine_table, slip_part, norming):
    part_real = (
        jnp.einsum("kx,cxz->kcz", cosine, slip_part, precision=lax.Precision.HIGHEST) * norming
    )
    part_imag = (
        -jnp.einsum("kx,cxz->kcz", sine_table, slip_part, precision=lax.Precision.HIGHEST) * norming
    )
    return jnp.stack([part_real, part_imag], 1)


def wave_sum(waves, places, spectrum, length, norming):
    cosine, sine_table = basis(waves, places, length)
    weights = jnp.where(waves == 0, 1.0, 2.0).astype(jnp.float32) * norming
    first_part = jnp.einsum(
        "kx,kcz->cxz", cosine * weights[:, None], spectrum[:, 0], precision=lax.Precision.HIGHEST
    )
    second_part = jnp.einsum(
        "kx,kcz->cxz",
        sine_table * weights[:, None],
        spectrum[:, 1],
        precision=lax.Precision.HIGHEST,
    )
    return first_part - second_part


def advance(
    disp_mid, vel_mid, dmg_mid, rate_mid, limit_mid, fault_mid, forces, energy, traction, signs
):
    pushes = traction[:, None, :, :, None] * signs[None] * fault_mid[None]
    vel_new = vel_mid + time_step * (forces + pushes)
    disp_new = disp_mid + time_step * vel_new
    dmg_new = 1.0 - (1.0 - dmg_mid) * jnp.exp(-rate_mid * jax.nn.softplus(energy - limit_mid))
    return (disp_new, vel_new, dmg_new)


def per_device(displacement, velocity, damage, material, damage_table, fault_rows, kernel, history):
    cells = displacement.shape[2]
    position = lax.axis_index("long")
    length = cells * lax.axis_size("long")
    owned = cells // 2
    norming = 1.0 / math.sqrt(length)
    rates = class_lookup(material, damage_table[0])
    limits = class_lookup(material, damage_table[1])
    heights = lax.broadcasted_iota(jnp.int32, damage.shape, 3)
    on_fault = (heights == fault_rows[..., None]).astype(displacement.dtype)
    signs = jnp.array([1.0, -1.0], displacement.dtype)[:, None, None, None]
    lagged = [history[level] for level in range(history.shape[0])]
    for number in range(STEPS):
        stiffness = 1.0 - damage
        stacked_fields = jnp.concatenate([displacement, stiffness[None]], 0)
        padded = padded_2(stacked_fields, (("long", 2),), 1)
        forces, energy = local_terms(padded[:-1], padded[-1])
        own_disp = displacement
        face = jnp.sum(own_disp * on_fault[None], axis=4)
        slip = face[:, 1] - face[:, 0]
        waves = jnp.arange(lax.axis_size("long") * owned, dtype=jnp.int32)
        places = position * cells + jnp.arange(cells, dtype=jnp.int32)
        cosine, sine_table = basis(waves, places, length)
        current = lax.psum_scatter(
            spectral_terms(cosine, sine_table, slip, norming),
            "long",
            scatter_dimension=0,
            tiled=True,
        )
        stacked_lags = jnp.stack([current] + lagged, 0)
        traction_real, traction_imag = convolve(kernel, stacked_lags)
        traction_spectrum = jnp.stack([traction_real, traction_imag], 1)

        def add_waves(piece):
            waves = jnp.arange(piece.shape[0], dtype=jnp.int32)
            places = position * cells + jnp.arange(cells, dtype=jnp.int32)
            return wave_sum(waves, places, piece, length, norming)

        traction = add_waves(lax.all_gather(traction_spectrum, "long", axis=0, tiled=True))
        displacement, velocity, damage = advance(
            displacement, velocity, damage, rates, limits, on_fault, forces, energy, traction, signs
        )
        lagged = [current] + lagged[:-1]
    return (displacement, velocity, damage, jnp.stack(lagged, 0))


def solution(mesh):
    placed = (
        P("groups", None, "long", None, None),
        P("groups", None, "long", None, None),
        P("groups", "long", None, None),
        P("groups", "long", None, None),
        P(),
        P("groups", "long", None),
        P(None, "long", None, None),
        P("groups", "long", None, None, None),
    )
    return jax.shard_map(
        per_device,
        mesh=mesh,
        in_specs=placed,
        out_specs=(
            P("groups", None, "long", None, None),
            P("groups", None, "long", None, None),
            P("groups", "long", None, None),
            P("groups", "long", None, None, None),
        ),
        check_vma=False,
    )
```

profile of v0, /device:TPU:0, one launch (start us, length us, event | category | flops | bytes accessed | tf_op | source)
XLA Modules:
  0.0 214.8 jit_solution(16481410820871778354)
XLA Ops:
  0.7 1.0 subtract_bitcast_fusion
  1.7 0.9 pad_maximum_fusion.31
  2.6 0.5 collective-permute-start
  3.1 5.1 %collective-permute-start.1 = (f32[3,2,1,16,256]{4,3,2,1,0:T(8,128)S(1)}, f32[3,2,1,16,256]{4,3,2,1,0:T(8,128)S(1)}, u32[]{:S(2)}, u32[]{:S(2)}) collective-permute-start(f32[3,2,1,16,256]{4,3,2,1,0:T(8,128)S(1)} %get-tuple-element.28), channel_id=1, source_target_pairs={{1,0},{2,1},{3,2},{4,3},{5,4},{6,5},{7,6},{8,7},{9,8},{10,9},{11,1... | collective-permute-start | bytes 294920 | tf_op jit(solution)/shard_map/ppermute | solution.py:20
  8.2 0.5 fusion.88
  8.8 0.7 fusion.127
  9.8 0.6 dynamic-slice
  11.0 0.5 select_maximum_fusion.3
  11.5 1.4 multiply_reduce_fusion.5
  12.9 0.2 fusion.7
  13.1 0.3 fusion.8
  13.5 0.7 fusion.38
  14.3 0.9 fusion.122
  15.2 0.1 copy.50
  15.3 62.3 %all-reduce.2 = f32[64,2,2,16]{3,2,1,0:T(2,128)S(1)} all-reduce(f32[64,2,2,16]{3,2,1,0:T(2,128)S(1)} %copy.50), channel_id=2, replica_groups=mesh['groups'=2,'long'=16] {'long'}, use_global_device_ids=true, to_apply=%region_1.2.clone | all-reduce | flops 4096 | bytes 32768
  77.6 0.2 subtract_reduce_fusion.1
  77.9 17.5 %all_gather.6 = f32[64,2,2,16]{3,2,1,0:T(2,128)S(1)} all-gather(f32[4,2,2,16]{3,2,1,0:T(2,128)S(1)} %copy.54), channel_id=1, replica_groups=mesh['groups'=2,'long'=16] {'long'}, dimensions={0}, use_global_device_ids=true | all-gather | bytes 17408 | tf_op jit(solution)/shard_map/all_gather | solution.py:151
  95.6 1.5 fusion.33
  97.1 0.3 fusion.48
  97.4 0.3 fusion.10
  97.8 6.1 %fusion.15 = (f32[2,8,16,256]{3,2,1,0:T(8,128)S(1)}, pred[2,8,16,256]{3,2,1,0:T(8,128)(4,1)}, pred[2,8,16,256]{3,2,1,0:T(8,128)(4,1)}, pred[2,8,16,256]{3,2,1,0:T(8,128)(4,1)}, pred[2,8,16,256]{3,2,1,0:T(8,128)(4,1)}) fusion(f32[2,8,16,256]{3,2,1,0:T(8,128)S(1)} %copy-done.5, f32[2,8,16,256]{3,2,1,0:T(8,128)S(1)} %copy-done.6, ...), kind=kLoop, calls=%fused_computation.57 | loop fusion | flops 2162688 | bytes 1835040 | tf_op jit(solution)/shard_map/sub | solution.py:126
  104.0 1.5 multiply_add_fusion.2
  105.5 0.4 collective-permute-start.2
  105.9 4.1 %collective-permute-start.3 = (f32[3,2,1,16,256]{4,3,2,1,0:T(8,128)S(1)}, f32[3,2,1,16,256]{4,3,2,1,0:T(8,128)S(1)}, u32[]{:S(2)}, u32[]{:S(2)}) collective-permute-start(f32[3,2,1,16,256]{4,3,2,1,0:T(8,128)S(1)} %get-tuple-element.26), channel_id=1, source_target_pairs={{1,0},{2,1},{3,2},{4,3},{5,4},{6,5},{7,6},{8,7},{9,8},{10,9},{11,1... | collective-permute-start | bytes 294920 | tf_op jit(solution)/shard_map/ppermute | solution.py:20
  110.0 0.6 slice.347
  110.7 1.8 collective-permute-done.2
  112.5 0.7 fusion.28
  113.2 0.9 multiply_reduce_fusion.2
  114.1 0.2 fusion.5
  114.4 0.3 fusion.4
  114.6 0.5 select_maximum_fusion
  115.1 1.3 multiply_reduce_fusion.1
  116.5 0.8 fusion.121
  117.2 0.8 copy.57
  118.0 63.8 %all-reduce.3 = f32[64,2,2,16]{3,2,1,0:T(2,128)} all-reduce(f32[64,2,2,16]{3,2,1,0:T(2,128)} %copy.57), channel_id=3, replica_groups=mesh['groups'=2,'long'=16] {'long'}, use_global_device_ids=true, to_apply=%region_8.9.clone | all-reduce | flops 4096 | bytes 32768
  181.8 0.7 dynamic-slice_bitcast_fusion
  182.5 0.2 subtract_reduce_fusion
  182.8 17.5 %all_gather.7 = f32[64,2,2,16]{3,2,1,0:T(2,128)S(1)} all-gather(f32[4,2,2,16]{3,2,1,0:T(2,128)S(1)} %copy.61), channel_id=1, replica_groups=mesh['groups'=2,'long'=16] {'long'}, dimensions={0}, use_global_device_ids=true | all-gather | bytes 17408 | tf_op jit(solution)/shard_map/all_gather | solution.py:151
  200.3 0.7 fusion.125
  200.9 0.9 copy.72
  201.8 0.9 fusion.45
  202.7 0.1 copy.73
  202.9 0.9 fusion.9
  203.8 0.1 broadcast_multiply_fusion
  203.9 1.7 pad_maximum_fusion.27
  205.6 1.3 fusion.23
  207.0 6.2 %fusion.19 = f32[2,8,16,256]{3,2,1,0:T(8,128)} fusion(f32[2,8,16,256]{3,2,1,0:T(8,128)S(1)} %get-tuple-element.18, f32[2,8,16,256]{3,2,1,0:T(8,128)S(1)} %copy-done.9, f32[2,8,16,256]{3,2,1,0:T(8,128)S(1)} %copy-done.10, f32[2,8,16,256]{3,2,1,0:T(8,128)S(1)} %copy-done.8, pred[2,8,16,256]{3,2,1,0:T(8,128)(4,1)S(1)} %copy-done.20, ...), kind=kLoop, calls=%fused_computation.61 | loop fusion | flops 1769472 | bytes 1572896 | tf_op jit(solution)/shard_map/sub | solution.py:109
  213.2 1.6 multiply_add_fusion
  (87 shorter events, 1.1 us)
Async XLA Ops:
  0.6 9.1 %copy-start.27 = (u32[32]{0:T(128)S(1)}, u32[32]{0:T(128)}, u32[]{:S(2)}) copy-start(u32[32]{0:T(128)} %constant.74) | copy-start | bytes 388
  0.6 10.4 %copy-start = (f32[2,2,8,16,256]{4,3,2,1,0:T(8,128)S(1)}, f32[2,2,8,16,256]{4,3,2,1,0:T(8,128)}, u32[]{:S(2)}) copy-start(f32[2,2,8,16,256]{4,3,2,1,0:T(8,128)} %param.9) | copy-start | bytes 1572868
  0.7 8.1 %copy-start.24 = (s32[2,8,16]{2,1,0:T(8,128)S(1)}, s32[2,8,16]{2,1,0:T(8,128)}, u32[]{:S(2)}) copy-start(s32[2,8,16]{2,1,0:T(8,128)} %param.14) | copy-start | bytes 3076
  0.7 8.2 %copy-start.23 = (f32[2,4]{1,0:T(2,128)S(1)}, f32[2,4]{1,0:T(2,128)}, u32[]{:S(2)}) copy-start(f32[2,4]{1,0:T(2,128)} %param.13) | copy-start | bytes 100
  0.7 8.8 %copy-start.25 = (f32[16,4,2,2]{0,3,2,1:T(2,128)S(1)}, f32[16,4,2,2]{0,3,2,1:T(2,128)}, u32[]{:S(2)}) copy-start(f32[16,4,2,2]{0,3,2,1:T(2,128)} %param.15) | copy-start | bytes 3076
  2.6 8.4 %collective-permute-start = (f32[3,2,1,16,256]{4,3,2,1,0:T(8,128)S(1)}, f32[3,2,1,16,256]{4,3,2,1,0:T(8,128)S(1)}, u32[]{:S(2)}, u32[]{:S(2)}) collective-permute-start(f32[3,2,1,16,256]{4,3,2,1,0:T(8,128)S(1)} %get-tuple-element.27), channel_id=1, source_target_pairs={{0,1},{1,2},{2,3},{3,4},{4,5},{5,6},{6,7},{7,8},{8,9},{9,10},{10,1... | collective-permute-start | bytes 294920 | tf_op jit(solution)/shard_map/ppermute | solution.py:17
  3.1 7.9 %collective-permute-start.1 = (f32[3,2,1,16,256]{4,3,2,1,0:T(8,128)S(1)}, f32[3,2,1,16,256]{4,3,2,1,0:T(8,128)S(1)}, u32[]{:S(2)}, u32[]{:S(2)}) collective-permute-start(f32[3,2,1,16,256]{4,3,2,1,0:T(8,128)S(1)} %get-tuple-element.28), channel_id=1, source_target_pairs={{1,0},{2,1},{3,2},{4,3},{5,4},{6,5},{7,6},{8,7},{9,8},{10,9},{11,1... | collective-permute-start | bytes 294920 | tf_op jit(solution)/shard_map/ppermute | solution.py:20
  9.7 67.9 %copy-start.14 = (f32[16,4,2]{2,1,0:T(4,128)}, f32[16,4,2]{2,1,0:T(4,128)S(1)}, u32[]{:S(2)}) copy-start(f32[16,4,2]{2,1,0:T(4,128)S(1)} %copy.53) | copy-start | bytes 1540
  13.5 64.1 %copy-start.11 = (f32[15,4,2,2,16]{4,3,2,1,0:T(2,128)S(1)}, f32[15,4,2,2,16]{4,3,2,1,0:T(2,128)}, u32[]{:S(2)}) copy-start(f32[15,4,2,2,16]{4,3,2,1,0:T(2,128)} %param.16) | copy-start | bytes 46084
  95.4 1.7 copy-start.28
  95.4 2.3 %copy-start.26 = (f32[2]{0:T(128)S(1)}, f32[2]{0:T(128)}, u32[]{:S(2)}) copy-start(f32[2]{0:T(128)} %constant.60.clone) | copy-start | bytes 28
  95.6 2.2 %copy-start.4 = (f32[2,8,16,256]{3,2,1,0:T(8,128)S(1)}, f32[2,8,16,256]{3,2,1,0:T(8,128)}, u32[]{:S(2)}) copy-start(f32[2,8,16,256]{3,2,1,0:T(8,128)} %get-tuple-element.6) | copy-start | bytes 786436
  95.6 2.2 %copy-start.5 = (f32[2,8,16,256]{3,2,1,0:T(8,128)S(1)}, f32[2,8,16,256]{3,2,1,0:T(8,128)}, u32[]{:S(2)}) copy-start(f32[2,8,16,256]{3,2,1,0:T(8,128)} %get-tuple-element.7) | copy-start | bytes 786436
  95.6 2.2 %copy-start.6 = (f32[2,8,16,256]{3,2,1,0:T(8,128)S(1)}, f32[2,8,16,256]{3,2,1,0:T(8,128)}, u32[]{:S(2)}) copy-start(f32[2,8,16,256]{3,2,1,0:T(8,128)} %get-tuple-element.62) | copy-start | bytes 786436
  95.6 2.2 %copy-start.7 = (f32[2,8,16,256]{3,2,1,0:T(8,128)S(1)}, f32[2,8,16,256]{3,2,1,0:T(8,128)}, u32[]{:S(2)}) copy-start(f32[2,8,16,256]{3,2,1,0:T(8,128)} %param.11) | copy-start | bytes 786436
  95.6 2.2 %copy-start.16 = (s32[2,8,16,256]{3,2,1,0:T(8,128)S(1)}, s32[2,8,16,256]{3,2,1,0:T(8,128)}, u32[]{:S(2)}) copy-start(s32[2,8,16,256]{3,2,1,0:T(8,128)} %param.12) | copy-start | bytes 786436
  97.1 6.9 %copy-start.3 = (f32[2,8,16,256]{3,2,1,0:T(8,128)S(1)}, f32[2,8,16,256]{3,2,1,0:T(8,128)}, u32[]{:S(2)}) copy-start(f32[2,8,16,256]{3,2,1,0:T(8,128)} %fusion.38) | copy-start | bytes 786436
  97.1 6.9 %copy-start.13 = (f32[2,2,8,16,256]{4,3,2,1,0:T(8,128)S(1)}, f32[2,2,8,16,256]{4,3,2,1,0:T(8,128)}, u32[]{:S(2)}) copy-start(f32[2,2,8,16,256]{4,3,2,1,0:T(8,128)} %param.10) | copy-start | bytes 1572868
  104.0 6.0 %copy-start.12 = (f32[15,4,2,2,16]{4,3,2,1,0:T(2,128)S(1)}, f32[15,4,2,2,16]{4,3,2,1,0:T(2,128)}, u32[]{:S(2)}) copy-start(f32[15,4,2,2,16]{4,3,2,1,0:T(2,128)} %param.16) | copy-start | bytes 46084
  105.5 6.9 %collective-permute-start.2 = (f32[3,2,1,16,256]{4,3,2,1,0:T(8,128)S(1)}, f32[3,2,1,16,256]{4,3,2,1,0:T(8,128)S(1)}, u32[]{:S(2)}, u32[]{:S(2)}) collective-permute-start(f32[3,2,1,16,256]{4,3,2,1,0:T(8,128)S(1)} %get-tuple-element.25), channel_id=1, source_target_pairs={{0,1},{1,2},{2,3},{3,4},{4,5},{5,6},{6,7},{7,8},{8,9},{9,10},{10,1... | collective-permute-start | bytes 294920 | tf_op jit(solution)/shard_map/ppermute | solution.py:17
  105.9 6.5 %collective-permute-start.3 = (f32[3,2,1,16,256]{4,3,2,1,0:T(8,128)S(1)}, f32[3,2,1,16,256]{4,3,2,1,0:T(8,128)S(1)}, u32[]{:S(2)}, u32[]{:S(2)}) collective-permute-start(f32[3,2,1,16,256]{4,3,2,1,0:T(8,128)S(1)} %get-tuple-element.26), channel_id=1, source_target_pairs={{1,0},{2,1},{3,2},{4,3},{5,4},{6,5},{7,6},{8,7},{9,8},{10,9},{11,1... | collective-permute-start | bytes 294920 | tf_op jit(solution)/shard_map/ppermute | solution.py:20
  112.5 3.9 %copy-start.21 = (f32[2,10,1,256]{3,2,1,0:T(1,128)}, f32[2,10,1,256]{3,2,1,0:T(1,128)S(1)}, u32[]{:S(2)}) copy-start(f32[2,10,1,256]{3,2,1,0:T(1,128)S(1)} %get-tuple-element.43) | copy-start | bytes 61444
  112.5 3.9 %copy-start.22 = (f32[2,10,1,256]{3,2,1,0:T(1,128)}, f32[2,10,1,256]{3,2,1,0:T(1,128)S(1)}, u32[]{:S(2)}) copy-start(f32[2,10,1,256]{3,2,1,0:T(1,128)S(1)} %get-tuple-element.44) | copy-start | bytes 61444
  116.4 66.1 %slice-start = ((f32[15,4,2,2,16]{4,3,2,1,0:T(2,128)}), f32[14,4,2,2,16]{4,3,2,1,0:T(2,128)S(1)}, s32[]{:S(2)}) async-start(f32[15,4,2,2,16]{4,3,2,1,0:T(2,128)} %param.16), calls=%async_computation | async-start | bytes 229376 | tf_op jit(solution)/shard_map/slice | solution.py:124
  116.4 66.2 %copy-start.15 = (f32[16,4,2]{2,1,0:T(4,128)S(1)}, f32[16,4,2]{2,1,0:T(4,128)}, u32[]{:S(2)}) copy-start(f32[16,4,2]{2,1,0:T(4,128)} %copy-done.14) | copy-start | bytes 1540
  203.9 3.1 %copy-start.8 = (f32[2,8,16,256]{3,2,1,0:T(8,128)S(1)}, f32[2,8,16,256]{3,2,1,0:T(8,128)}, u32[]{:S(2)}) copy-start(f32[2,8,16,256]{3,2,1,0:T(8,128)} %get-tuple-element.4) | copy-start | bytes 786436
  203.9 3.1 %copy-start.9 = (f32[2,8,16,256]{3,2,1,0:T(8,128)S(1)}, f32[2,8,16,256]{3,2,1,0:T(8,128)}, u32[]{:S(2)}) copy-start(f32[2,8,16,256]{3,2,1,0:T(8,128)} %get-tuple-element.5) | copy-start | bytes 786436
  203.9 3.1 %copy-start.10 = (f32[2,8,16,256]{3,2,1,0:T(8,128)S(1)}, f32[2,8,16,256]{3,2,1,0:T(8,128)}, u32[]{:S(2)}) copy-start(f32[2,8,16,256]{3,2,1,0:T(8,128)} %get-tuple-element.8) | copy-start | bytes 786436
  203.9 3.1 %copy-start.17 = (pred[2,8,16,256]{3,2,1,0:T(8,128)(4,1)S(1)}, pred[2,8,16,256]{3,2,1,0:T(8,128)(4,1)}, u32[]{:S(2)}) copy-start(pred[2,8,16,256]{3,2,1,0:T(8,128)(4,1)} %get-tuple-element.19) | copy-start | bytes 196612
  203.9 3.1 %copy-start.18 = (pred[2,8,16,256]{3,2,1,0:T(8,128)(4,1)S(1)}, pred[2,8,16,256]{3,2,1,0:T(8,128)(4,1)}, u32[]{:S(2)}) copy-start(pred[2,8,16,256]{3,2,1,0:T(8,128)(4,1)} %get-tuple-element.20) | copy-start | bytes 196612
  203.9 3.1 %copy-start.19 = (pred[2,8,16,256]{3,2,1,0:T(8,128)(4,1)S(1)}, pred[2,8,16,256]{3,2,1,0:T(8,128)(4,1)}, u32[]{:S(2)}) copy-start(pred[2,8,16,256]{3,2,1,0:T(8,128)(4,1)} %get-tuple-element.21) | copy-start | bytes 196612
  203.9 3.1 %copy-start.20 = (pred[2,8,16,256]{3,2,1,0:T(8,128)(4,1)S(1)}, pred[2,8,16,256]{3,2,1,0:T(8,128)(4,1)}, u32[]{:S(2)}) copy-start(pred[2,8,16,256]{3,2,1,0:T(8,128)(4,1)} %get-tuple-element.22) | copy-start | bytes 196612
  206.9 6.3 %copy-start.1 = (f32[2,2,8,16,256]{4,3,2,1,0:T(8,128)S(1)}, f32[2,2,8,16,256]{4,3,2,1,0:T(8,128)}, u32[]{:S(2)}) copy-start(f32[2,2,8,16,256]{4,3,2,1,0:T(8,128)} %get-tuple-element.24) | copy-start | bytes 1572868
  207.0 6.3 %copy-start.2 = (f32[2,8,16,256]{3,2,1,0:T(8,128)S(1)}, f32[2,8,16,256]{3,2,1,0:T(8,128)}, u32[]{:S(2)}) copy-start(f32[2,8,16,256]{3,2,1,0:T(8,128)} %fusion.28) | copy-start | bytes 786436
where the time goes:
time: 215 us
  blocking collectives  161 us (75%)
  other arithmetic  29.3 us (14%)
  starting transfers between devices  10.1 us (5%)
  local copies, waits for them, and re-layouts  7.45 us (3%)
  matrix products  3.4 us (2%)
    unnamed x2, blocking collectives  126 us
    all_gather x2, blocking collectives, per_device(): lax.all_gather(traction_spectrum, 'long', axis=0, tiled=True)  35 us
    ppermute x2, starting transfers between devices, padded_2(): lax.ppermute(lax.slice_in_dim(block, 0, width, axis=dim), axis, backward)  9.16 us
    sub x1, other arithmetic, advance(): 1.0 - (1.0 - dmg_mid) * jnp.exp(-rate_mid * jax.nn.softplus(energy - limi...  6.16 us
    sub x1, other arithmetic, per_device(): stiffness = 1.0 - damage  6.15 us
  transfers between devices with their start and end apart: 4, of which 1 were waited for; matrix products, arithmetic and copies ran while one was open for 1% of the time, Pallas kernels for 0%

commit v1 on v0

--- a/solution.py
+++ b/solution.py
@@ -6,6 +6,18 @@
 
 STEPS = 2
 time_step = 0.5
+
+
+def collect(x, axis, dim):
+    ways, here = (lax.axis_size(axis), lax.axis_index(axis))
+    grown, reach = (x, 1)
+    while reach < ways:
+        theirs = lax.ppermute(grown, axis, [(d, d ^ reach) for d in range(ways)])
+        mine_first = jnp.concatenate([grown, theirs], axis=dim)
+        theirs_first = jnp.concatenate([theirs, grown], axis=dim)
+        grown = jnp.where(here & reach == 0, mine_first, theirs_first)
+        reach = 2 * reach
+    return grown
 
 
 def padded_2(block, sides, width):
@@ -148,7 +160,7 @@
             places = position * cells + jnp.arange(cells, dtype=jnp.int32)
             return wave_sum(waves, places, piece, length, norming)
 
-        traction = add_waves(lax.all_gather(traction_spectrum, "long", axis=0, tiled=True))
+        traction = add_waves(collect(traction_spectrum, "long", 0))
         displacement, velocity, damage = advance(
             displacement, velocity, damage, rates, limits, on_fault, forces, energy, traction, signs
         )

time: 215 us -> 191 us (0.89)
  blocking collectives: 161 us -> 125 us
  waiting for transfers between devices: 1.76 us -> 22.3 us
  local copies, waits for them, and re-layouts: 7.45 us -> 2.75 us
  other arithmetic: 29.3 us -> 25.7 us
    all_gather x2 -> x0, blocking collectives: 35 us -> none  [per_device(): lax.all_gather(traction_spectrum, 'long', axis=0, tiled=True)]
    ppermute x0 -> x8, waiting for transfers between devices: none -> 20 us  [collect(): theirs = lax.ppermute(grown, axis, [(d, d ^ reach) for d in range(ways)])]
  transfers between devices with their start and end apart: 4 -> 12, of which waited for: 1 -> 6; matrix products, arithmetic and copies ran while one was open for 1% -> 10% of each run, Pallas kernels for 0% -> 0%
where the time goes in v1:
time: 191 us; the launch traced here: 190 us
  blocking collectives  125 us (65%)
  other arithmetic  25.7 us (13%)
  waiting for transfers between devices  22.3 us (12%)
  starting transfers between devices  10.6 us (6%)
  local copies, waits for them, and re-layouts  2.75 us (1%)
  matrix products  2.18 us (1%)
  between operations  1.96 us (1%)
    unnamed x2, blocking collectives  125 us
    ppermute x8, waiting for transfers between devices, collect(): theirs = lax.ppermute(grown, axis, [(d, d ^ reach) for d in range(ways)])  20 us
    ppermute x2, starting transfers between devices, padded_2(): lax.ppermute(lax.slice_in_dim(block, 0, width, axis=dim), axis, backward)  9.49 us
    sub x1, other arithmetic, per_device(): stiffness = 1.0 - damage  7.59 us
    sub x1, other arithmetic, advance(): 1.0 - (1.0 - dmg_mid) * jnp.exp(-rate_mid * jax.nn.softplus(energy - limi...  6.35 us
  transfers between devices with their start and end apart: 12, of which 6 were waited for; matrix products, arithmetic and copies ran while one was open for 10% of the time, Pallas kernels for 0%

profile of v1, /device:TPU:0, one launch (start us, length us, event | category | flops | bytes accessed | tf_op | source)
XLA Modules:
  0.0 190.5 jit_solution(17013212001108436277)
XLA Ops:
  0.7 1.0 subtract_bitcast_fusion
  1.7 0.9 pad_maximum_fusion.31
  2.6 0.5 collective-permute-start
  3.1 5.1 %collective-permute-start.1 = (f32[3,2,1,16,256]{4,3,2,1,0:T(8,128)S(1)}, f32[3,2,1,16,256]{4,3,2,1,0:T(8,128)S(1)}, u32[]{:S(2)}, u32[]{:S(2)}) collective-permute-start(f32[3,2,1,16,256]{4,3,2,1,0:T(8,128)S(1)} %get-tuple-element.28), channel_id=1, source_target_pairs={{1,0},{2,1},{3,2},{4,3},{5,4},{6,5},{7,6},{8,7},{9,8},{10,9},{11,1... | collective-permute-start | bytes 294920 | tf_op jit(solution)/shard_map/ppermute | solution.py:32
  8.2 0.6 fusion.84
  8.8 0.1 fusion.40
  8.9 0.7 fusion.121
  9.6 0.1 copy.49
  9.7 0.1 copy.53
  9.8 0.6 dynamic-slice
  11.1 0.5 select_maximum_fusion.3
  11.6 1.4 multiply_reduce_fusion.5
  12.9 0.2 fusion.7
  13.2 0.3 fusion.8
  13.6 0.1 copy.50
  13.7 62.1 %all-reduce.2 = f32[64,2,2,16]{3,2,1,0:T(2,128)S(1)} all-reduce(f32[64,2,2,16]{3,2,1,0:T(2,128)S(1)} %copy.50), channel_id=2, replica_groups=mesh['groups'=2,'long'=16] {'long'}, use_global_device_ids=true, to_apply=%region_1.2.clone | all-reduce | flops 4096 | bytes 32768
  75.9 0.2 subtract_reduce_fusion.1
  76.1 0.1 copy.54
  76.4 7.6 %fusion.15 = (f32[2,8,16,256]{3,2,1,0:T(8,128)S(1)}, pred[2,8,16,256]{3,2,1,0:T(8,128)(4,1)}, pred[2,8,16,256]{3,2,1,0:T(8,128)(4,1)}, pred[2,8,16,256]{3,2,1,0:T(8,128)(4,1)}, pred[2,8,16,256]{3,2,1,0:T(8,128)(4,1)}) fusion(f32[2,8,16,256]{3,2,1,0:T(8,128)} %get-tuple-element.7, f32[2,8,16,256]{3,2,1,0:T(8,128)} %get-tuple-element.58, ...), kind=kLoop, calls=%fused_computation.57 | loop fusion | flops 2162688 | bytes 1835040 | tf_op jit(solution)/shard_map/sub | solution.py:138
  84.2 0.1 fusion.118
  84.3 3.8 %collective-permute-done.3 = f32[8,2,2,16]{0,3,2,1:T(8,128)S(1)} collective-permute-done((f32[8,2,2,16]{0,3,2,1:T(8,128)S(1)}, f32[8,2,2,16]{0,3,2,1:T(8,128)S(1)}, u32[]{:S(2)}, u32[]{:S(2)}) %collective-permute-start.3) | collective-permute-done | bytes 2080 | tf_op jit(solution)/shard_map/ppermute | solution.py:15
  88.3 0.3 fusion.33
  88.7 3.5 %collective-permute-done.4 = f32[16,2,2,16]{0,3,2,1:T(8,128)S(1)} collective-permute-done((f32[16,2,2,16]{0,3,2,1:T(8,128)S(1)}, f32[16,2,2,16]{0,3,2,1:T(8,128)S(1)}, u32[]{:S(2)}, u32[]{:S(2)}) %collective-permute-start.4) | collective-permute-done | bytes 4128 | tf_op jit(solution)/shard_map/ppermute | solution.py:15
  92.4 4.8 %collective-permute-done.5 = f32[32,2,2,16]{0,3,2,1:T(8,128)S(1)} collective-permute-done((f32[32,2,2,16]{0,3,2,1:T(8,128)S(1)}, f32[32,2,2,16]{0,3,2,1:T(8,128)S(1)}, u32[]{:S(2)}, u32[]{:S(2)}) %collective-permute-start.5) | collective-permute-done | bytes 8224 | tf_op jit(solution)/shard_map/ppermute | solution.py:15
  97.3 0.3 fusion.45
  97.5 0.3 fusion.10
  98.0 1.5 multiply_add_fusion.2
  99.6 4.4 %collective-permute-start.7 = (f32[3,2,1,16,256]{4,3,2,1,0:T(8,128)S(1)}, f32[3,2,1,16,256]{4,3,2,1,0:T(8,128)S(1)}, u32[]{:S(2)}, u32[]{:S(2)}) collective-permute-start(f32[3,2,1,16,256]{4,3,2,1,0:T(8,128)S(1)} %get-tuple-element.26), channel_id=1, source_target_pairs={{1,0},{2,1},{3,2},{4,3},{5,4},{6,5},{7,6},{8,7},{9,8},{10,9},{11,1... | collective-permute-start | bytes 294920 | tf_op jit(solution)/shard_map/ppermute | solution.py:32
  104.0 2.3 %collective-permute-done.6 = f32[3,2,1,16,256]{4,3,2,1,0:T(8,128)S(1)} collective-permute-done((f32[3,2,1,16,256]{4,3,2,1,0:T(8,128)S(1)}, f32[3,2,1,16,256]{4,3,2,1,0:T(8,128)S(1)}, u32[]{:S(2)}, u32[]{:S(2)}) %collective-permute-start.6) | collective-permute-done | bytes 98336 | tf_op jit(solution)/shard_map/ppermute | solution.py:29
  106.3 0.2 multiply_reduce_fusion.2
  106.5 0.3 fusion.5
  106.7 0.3 fusion.4
  107.2 0.1 fusion.117
  107.3 0.1 copy.56
  107.4 62.8 %all-reduce.3 = f32[64,2,2,16]{3,2,1,0:T(2,128)S(1)} all-reduce(f32[64,2,2,16]{3,2,1,0:T(2,128)S(1)} %copy.56), channel_id=3, replica_groups=mesh['groups'=2,'long'=16] {'long'}, use_global_device_ids=true, to_apply=%region_8.9.clone | all-reduce | flops 4096 | bytes 32768
  170.4 0.2 subtract_reduce_fusion
  170.6 0.1 copy.60
  170.9 0.3 fusion.23
  171.2 0.5 select_maximum_fusion
  171.7 0.5 multiply_reduce_fusion.1
  172.4 0.1 copy-done.6
  172.6 6.4 %fusion.19 = f32[2,8,16,256]{3,2,1,0:T(8,128)} fusion(f32[2,8,16,256]{3,2,1,0:T(8,128)S(1)} %get-tuple-element.18, f32[2,8,16,256]{3,2,1,0:T(8,128)S(1)} %get-tuple-element.5, f32[2,8,16,256]{3,2,1,0:T(8,128)S(1)} %get-tuple-element.8, f32[2,8,16,256]{3,2,1,0:T(8,128)S(1)} %get-tuple-element.4, pred[2,8,16,256]{3,2,1,0:T(8,128)(4,1)S(1)} %copy-done.9, ...), kind=kLoop, calls=%fused_computation.61 | loop fusion | flops 1769472 | bytes 1572896 | tf_op jit(solution)/shard_map/sub | solution.py:121
  179.2 3.9 %collective-permute-done.10 = f32[16,2,2,16]{0,3,2,1:T(8,128)S(1)} collective-permute-done((f32[16,2,2,16]{0,3,2,1:T(8,128)S(1)}, f32[16,2,2,16]{0,3,2,1:T(8,128)S(1)}, u32[]{:S(2)}, u32[]{:S(2)}) %collective-permute-start.10) | collective-permute-done | bytes 4128 | tf_op jit(solution)/shard_map/ppermute | solution.py:15
  183.2 0.7 pad_maximum_fusion.27
  183.9 4.1 %collective-permute-done.11 = f32[32,2,2,16]{0,3,2,1:T(8,128)S(1)} collective-permute-done((f32[32,2,2,16]{0,3,2,1:T(8,128)S(1)}, f32[32,2,2,16]{0,3,2,1:T(8,128)S(1)}, u32[]{:S(2)}, u32[]{:S(2)}) %collective-permute-start.11) | collective-permute-done | bytes 8224 | tf_op jit(solution)/shard_map/ppermute | solution.py:15
  188.1 0.3 fusion.44
  188.4 0.3 fusion.9
  188.8 1.7 multiply_add_fusion
  (82 shorter events, 2.3 us)
Async XLA Ops:
  0.6 9.2 %copy-start.14 = (u32[32]{0:T(128)S(1)}, u32[32]{0:T(128)}, u32[]{:S(2)}) copy-start(u32[32]{0:T(128)} %constant.78) | copy-start | bytes 388
  0.6 10.4 %copy-start = (f32[2,2,8,16,256]{4,3,2,1,0:T(8,128)S(1)}, f32[2,2,8,16,256]{4,3,2,1,0:T(8,128)}, u32[]{:S(2)}) copy-start(f32[2,2,8,16,256]{4,3,2,1,0:T(8,128)} %param.9) | copy-start | bytes 1572868
  0.7 8.1 %copy-start.11 = (s32[2,8,16]{2,1,0:T(8,128)S(1)}, s32[2,8,16]{2,1,0:T(8,128)}, u32[]{:S(2)}) copy-start(s32[2,8,16]{2,1,0:T(8,128)} %param.14) | copy-start | bytes 3076
  0.7 8.2 %copy-start.10 = (f32[2,4]{1,0:T(2,128)S(1)}, f32[2,4]{1,0:T(2,128)}, u32[]{:S(2)}) copy-start(f32[2,4]{1,0:T(2,128)} %param.13) | copy-start | bytes 100
  0.7 8.9 %copy-start.12 = (f32[16,4,2,2]{0,3,2,1:T(2,128)S(1)}, f32[16,4,2,2]{0,3,2,1:T(2,128)}, u32[]{:S(2)}) copy-start(f32[16,4,2,2]{0,3,2,1:T(2,128)} %param.15) | copy-start | bytes 3076
  2.6 8.5 %collective-permute-start = (f32[3,2,1,16,256]{4,3,2,1,0:T(8,128)S(1)}, f32[3,2,1,16,256]{4,3,2,1,0:T(8,128)S(1)}, u32[]{:S(2)}, u32[]{:S(2)}) collective-permute-start(f32[3,2,1,16,256]{4,3,2,1,0:T(8,128)S(1)} %get-tuple-element.27), channel_id=1, source_target_pairs={{0,1},{1,2},{2,3},{3,4},{4,5},{5,6},{6,7},{7,8},{8,9},{9,10},{10,1... | collective-permute-start | bytes 294920 | tf_op jit(solution)/shard_map/ppermute | solution.py:29
  3.1 8.0 %collective-permute-start.1 = (f32[3,2,1,16,256]{4,3,2,1,0:T(8,128)S(1)}, f32[3,2,1,16,256]{4,3,2,1,0:T(8,128)S(1)}, u32[]{:S(2)}, u32[]{:S(2)}) collective-permute-start(f32[3,2,1,16,256]{4,3,2,1,0:T(8,128)S(1)} %get-tuple-element.28), channel_id=1, source_target_pairs={{1,0},{2,1},{3,2},{4,3},{5,4},{6,5},{7,6},{8,7},{9,8},{10,9},{11,1... | collective-permute-start | bytes 294920 | tf_op jit(solution)/shard_map/ppermute | solution.py:32
  9.8 66.1 %copy-start.4 = (f32[16,4,2]{2,1,0:T(4,128)}, f32[16,4,2]{2,1,0:T(4,128)S(1)}, u32[]{:S(2)}) copy-start(f32[16,4,2]{2,1,0:T(4,128)S(1)} %copy.53) | copy-start | bytes 1540
  12.9 62.9 %copy-start.2 = (f32[15,4,2,2,16]{4,3,2,1,0:T(2,128)S(1)}, f32[15,4,2,2,16]{4,3,2,1,0:T(2,128)}, u32[]{:S(2)}) copy-start(f32[15,4,2,2,16]{4,3,2,1,0:T(2,128)} %param.16) | copy-start | bytes 46084
  76.3 7.8 %collective-permute-start.2 = (f32[4,2,2,16]{0,3,2,1:T(8,128)S(1)}, f32[4,2,2,16]{0,3,2,1:T(8,128)S(1)}, u32[]{:S(2)}, u32[]{:S(2)}) collective-permute-start(f32[4,2,2,16]{0,3,2,1:T(8,128)S(1)} %pad_maximum_fusion.34), channel_id=1, source_target_pairs={{0,1},{1,0},{2,3},{3,2},{4,5},{5,4},{6,7},{7,6},{8,9},{9,8},{10,11... | collective-permute-start | bytes 3080 | tf_op jit(solution)/shard_map/ppermute | solution.py:15
  84.1 4.0 %collective-permute-start.3 = (f32[8,2,2,16]{0,3,2,1:T(8,128)S(1)}, f32[8,2,2,16]{0,3,2,1:T(8,128)S(1)}, u32[]{:S(2)}, u32[]{:S(2)}) collective-permute-start(f32[8,2,2,16]{0,3,2,1:T(8,128)S(1)} %maximum_select_fusion), channel_id=1, source_target_pairs={{0,2},{1,3},{2,0},{3,1},{4,6},{5,7},{6,4},{7,5},{8,10},{9,11},{10,... | collective-permute-start | bytes 6152 | tf_op jit(solution)/shard_map/ppermute | solution.py:15
  88.2 4.0 %collective-permute-start.4 = (f32[16,2,2,16]{0,3,2,1:T(8,128)S(1)}, f32[16,2,2,16]{0,3,2,1:T(8,128)S(1)}, u32[]{:S(2)}, u32[]{:S(2)}) collective-permute-start(f32[16,2,2,16]{0,3,2,1:T(8,128)S(1)} %maximum_select_fusion.1), channel_id=1, source_target_pairs={{0,4},{1,5},{2,6},{3,7},{4,0},{5,1},{6,2},{7,3},{8,12},{9,13},{10,... | collective-permute-start | bytes 12296 | tf_op jit(solution)/shard_map/ppermute | solution.py:15
  88.3 9.0 %copy-start.15 = (f32[64]{0:T(128)S(1)}, f32[64]{0:T(128)}, u32[]{:S(2)}) copy-start(f32[64]{0:T(128)} %fusion.84) | copy-start | bytes 772
  88.3 9.6 %copy-start.13 = (f32[2]{0:T(128)S(1)}, f32[2]{0:T(128)}, u32[]{:S(2)}) copy-start(f32[2]{0:T(128)} %constant.64.clone) | copy-start | bytes 28
  88.3 9.7 %copy-start.3 = (f32[2,2,8,16,256]{4,3,2,1,0:T(8,128)S(1)}, f32[2,2,8,16,256]{4,3,2,1,0:T(8,128)}, u32[]{:S(2)}) copy-start(f32[2,2,8,16,256]{4,3,2,1,0:T(8,128)} %param.10) | copy-start | bytes 1572868
  92.3 4.9 %collective-permute-start.5 = (f32[32,2,2,16]{0,3,2,1:T(8,128)S(1)}, f32[32,2,2,16]{0,3,2,1:T(8,128)S(1)}, u32[]{:S(2)}, u32[]{:S(2)}) collective-permute-start(f32[32,2,2,16]{0,3,2,1:T(8,128)S(1)} %maximum_select_fusion.2), channel_id=1, source_target_pairs={{0,8},{1,9},{2,10},{3,11},{4,12},{5,13},{6,14},{7,15},{8,0},{9,1},... | collective-permute-start | bytes 24584 | tf_op jit(solution)/shard_map/ppermute | solution.py:15
  99.5 6.8 %collective-permute-start.6 = (f32[3,2,1,16,256]{4,3,2,1,0:T(8,128)S(1)}, f32[3,2,1,16,256]{4,3,2,1,0:T(8,128)S(1)}, u32[]{:S(2)}, u32[]{:S(2)}) collective-permute-start(f32[3,2,1,16,256]{4,3,2,1,0:T(8,128)S(1)} %get-tuple-element.25), channel_id=1, source_target_pairs={{0,1},{1,2},{2,3},{3,4},{4,5},{5,6},{6,7},{7,8},{8,9},{9,10},{10,1... | collective-permute-start | bytes 294920 | tf_op jit(solution)/shard_map/ppermute | solution.py:29
  99.6 6.7 %collective-permute-start.7 = (f32[3,2,1,16,256]{4,3,2,1,0:T(8,128)S(1)}, f32[3,2,1,16,256]{4,3,2,1,0:T(8,128)S(1)}, u32[]{:S(2)}, u32[]{:S(2)}) collective-permute-start(f32[3,2,1,16,256]{4,3,2,1,0:T(8,128)S(1)} %get-tuple-element.26), channel_id=1, source_target_pairs={{1,0},{2,1},{3,2},{4,3},{5,4},{6,5},{7,6},{8,7},{9,8},{10,9},{11,1... | collective-permute-start | bytes 294920 | tf_op jit(solution)/shard_map/ppermute | solution.py:32
  107.0 63.3 %slice-start = ((f32[15,4,2,2,16]{4,3,2,1,0:T(2,128)}), f32[14,4,2,2,16]{4,3,2,1,0:T(2,128)S(1)}, s32[]{:S(2)}) async-start(f32[15,4,2,2,16]{4,3,2,1,0:T(2,128)} %param.16), calls=%async_computation | async-start | bytes 229376 | tf_op jit(solution)/shard_map/slice | solution.py:136
  107.0 63.3 %copy-start.5 = (f32[16,4,2]{2,1,0:T(4,128)S(1)}, f32[16,4,2]{2,1,0:T(4,128)}, u32[]{:S(2)}) copy-start(f32[16,4,2]{2,1,0:T(4,128)} %copy-done.4) | copy-start | bytes 1540
  170.8 1.4 collective-permute-start.8
  171.7 0.8 copy-start.6
  171.7 0.9 copy-start.7
  171.7 0.9 copy-start.8
  171.7 0.9 copy-start.9
  172.2 11.0 %slice-start.1 = ((f32[15,4,2,2,16]{4,3,2,1,0:T(2,128)}), f32[13,4,2,2,16]{4,3,2,1,0:T(2,128)S(1)}, s32[]{:S(2)}) async-start(f32[15,4,2,2,16]{4,3,2,1,0:T(2,128)} %param.16), calls=%async_computation.1 | async-start | bytes 212992 | tf_op jit(solution)/shard_map/slice | solution.py:136
  172.3 15.8 %copy-start.16 = (f32[64]{0:T(128)S(1)}, f32[64]{0:T(128)}, u32[]{:S(2)}) copy-start(f32[64]{0:T(128)} %fusion.84) | copy-start | bytes 772
  172.3 6.6 %collective-permute-start.9 = (f32[8,2,2,16]{0,3,2,1:T(8,128)S(1)}, f32[8,2,2,16]{0,3,2,1:T(8,128)S(1)}, u32[]{:S(2)}, u32[]{:S(2)}) collective-permute-start(f32[8,2,2,16]{0,3,2,1:T(8,128)S(1)} %maximum_select_fusion.4), channel_id=1, source_target_pairs={{0,2},{1,3},{2,0},{3,1},{4,6},{5,7},{6,4},{7,5},{8,10},{9,11},{10,... | collective-permute-start | bytes 6152 | tf_op jit(solution)/shard_map/ppermute | solution.py:15
  172.6 16.2 %copy-start.1 = (f32[2,2,8,16,256]{4,3,2,1,0:T(8,128)S(1)}, f32[2,2,8,16,256]{4,3,2,1,0:T(8,128)}, u32[]{:S(2)}) copy-start(f32[2,2,8,16,256]{4,3,2,1,0:T(8,128)} %get-tuple-element.24) | copy-start | bytes 1572868
  179.1 4.0 %collective-permute-start.10 = (f32[16,2,2,16]{0,3,2,1:T(8,128)S(1)}, f32[16,2,2,16]{0,3,2,1:T(8,128)S(1)}, u32[]{:S(2)}, u32[]{:S(2)}) collective-permute-start(f32[16,2,2,16]{0,3,2,1:T(8,128)S(1)} %maximum_select_fusion.5), channel_id=1, source_target_pairs={{0,4},{1,5},{2,6},{3,7},{4,0},{5,1},{6,2},{7,3},{8,12},{9,13},{10,... | collective-permute-start | bytes 12296 | tf_op jit(solution)/shard_map/ppermute | solution.py:15
  183.1 4.9 %collective-permute-start.11 = (f32[32,2,2,16]{0,3,2,1:T(8,128)S(1)}, f32[32,2,2,16]{0,3,2,1:T(8,128)S(1)}, u32[]{:S(2)}, u32[]{:S(2)}) collective-permute-start(f32[32,2,2,16]{0,3,2,1:T(8,128)S(1)} %maximum_select_fusion.6), channel_id=1, source_target_pairs={{0,8},{1,9},{2,10},{3,11},{4,12},{5,13},{6,14},{7,15},{8,0},{9,1},... | collective-permute-start | bytes 24584 | tf_op jit(solution)/shard_map/ppermute | solution.py:15
